TPU v7x, 32 devices: a whole 2x2x4 slice. The times are simulated.
32 devices in a mesh: row: 8 (over y, x, core), col: 4 (over z).
Axes of the slice: x: 2, y: 2, z: 4, core: 2. Of those that a mesh axis runs over, the one named last changes fastest.
Arguments:
- features: bfloat16 [1024, 4, 512], P('row', 'col'), may hold values from -6 to 6
- adj_blocks: bfloat16 [8, 4, 128, 128, 128], P('row', 'col'), may hold values from -0.0625 to 0.0625
- block_rows: int32 [8, 4, 128], P('row', 'col'), may hold values from 0 to 3
- block_cols: int32 [8, 4, 128], P('row', 'col'), may hold values from 0 to 7
- block_counts: int32 [8, 4], P('row', 'col'), may hold values from 16 to 128, as said below
- w_qkv: bfloat16 [512, 1536], replicated, may hold values from -0.25 to 0.25
Outputs:
- aggregated: bfloat16 [4096, 512], P(('row', 'col'))
- qkv: bfloat16 [4096, 1536], P(('row', 'col'))
Inputs may be any that keep to these rules, and one draw needn't show every extreme that they name: `block_counts`: some tile has exactly 128 live slots and some exactly 16.
All inputs are finite; a program needn't handle non-finite values.
Results may differ from a plain program's by a relative error of at most 0.012.
Values may be sent and summed in bfloat16 or wider, within the bound.
A program may use at most 128 MiB of HBM per device.

v0:
```python
import jax
import jax.numpy as jnp
from jax import lax
from jax.sharding import PartitionSpec as P


def group_size():
    size_now = 1
    for candidate in (2, 4, 8, 16, 32):
        size_now = candidate
    return size_now


def accumulate(tile_blocks, row_ids, live_mask, feats_of, carry):
    slot_total = tile_blocks.shape[0]
    step_size = group_size()
    turns = slot_total // step_size
    grouped_blocks = tile_blocks.reshape(
        turns, step_size, tile_blocks.shape[1], tile_blocks.shape[2]
    )
    grouped_rows = row_ids.reshape(turns, step_size)
    grouped_mask = live_mask.reshape(turns, step_size)
    grouped_index = jnp.arange(slot_total, dtype=jnp.int32).reshape(turns, step_size)

    def one_group(partial_value, inputs):
        blocks_now, rows_now, mask_now, index_now = inputs
        block_feats = feats_of(index_now)
        products = jnp.einsum(
            "gij,gjf->gif", blocks_now, block_feats, preferred_element_type=jnp.float32
        )
        products = jnp.where(mask_now[:, None, None], products, jnp.float32(0.0))
        return (partial_value.at[rows_now].add(products), None)

    result, unused = lax.scan(
        one_group, carry, (grouped_blocks, grouped_rows, grouped_mask, grouped_index)
    )
    return result


def body(features, adj_blocks, block_rows, block_cols, block_counts, w_qkv):
    tile_blocks = adj_blocks[0, 0]
    row_ids = block_rows[0, 0]
    col_ids = block_cols[0, 0]
    live_count = block_counts[0, 0]
    cell_dev = features.shape[0]
    feat_width = features.shape[2]
    slot_total = tile_blocks.shape[0]
    block_side = tile_blocks.shape[1]
    tile_cells = cell_dev * lax.axis_size("col")
    block_rows_total = tile_cells // block_side
    slot_index = jnp.arange(slot_total, dtype=jnp.int32)
    live_mask = slot_index < live_count
    start_sum = jnp.zeros((block_rows_total, block_side, feat_width), jnp.float32)
    gathered = lax.all_gather(features, "row", axis=0, tiled=True)
    panel_blocks = gathered[:, 0, :].reshape(-1, block_side, feat_width)

    def feats_whole(index_now):
        return jnp.take(panel_blocks, col_ids[index_now], axis=0)

    partial_value = accumulate(tile_blocks, row_ids, live_mask, feats_whole, start_sum)
    partial_rows = partial_value.reshape(tile_cells, feat_width)
    summed = lax.psum_scatter(
        partial_rows.astype(jnp.bfloat16), "col", scatter_dimension=0, tiled=True
    )
    qkv = jnp.dot(summed, w_qkv, preferred_element_type=jnp.float32).astype(jnp.bfloat16)
    return (summed, qkv)


def solution(mesh):
    placed = (
        P("row", "col", None),
        P("row", "col", None, None, None),
        P("row", "col", None),
        P("row", "col", None),
        P("row", "col"),
        P(),
    )
    return jax.shard_map(
        body,
        mesh=mesh,
        in_specs=placed,
        out_specs=(P(("row", "col"), None), P(("row", "col"), None)),
        check_vma=False,
    )
```

profile of v0, /device:TPU:0, one launch (start us, length us, event | category | flops | bytes accessed | tf_op | source)
XLA Modules:
  0.0 164.5 jit_solution(16068252825244014125)
XLA Ops:
  7.2 0.0 copy-start
  7.2 0.0 all-gather.2.cloned.1.call-start
  7.2 0.7 all-gather.2.cloned.1.call-update
  7.9 0.0 reduce-scatter.2.cloned.1.call-start
  8.0 0.5 broadcast.84
  8.5 1.3 reduce.3
  9.8 0.1 reshape_squeeze.9
  10.6 25.6 %all-gather.2.cloned.1.call-done = bf16[1024,1,512]{2,0,1:T(8,128)(2,1)} async-done(((bf16[128,1,512]{2,0,1:T(8,128)(2,1)}), bf16[1024,1,512]{2,0,1:T(8,128)(2,1)}) %all-gather.2.cloned.1.call-update) | async-done | bytes 1048592 | tf_op jit(solution)/shard_map/all_gather | solution.py:54
  36.1 0.1 broadcast_in_dim.30
  36.2 96.8 %while.10 = (s32[]{:T(128)}, f32[4,128,512]{2,1,0:T(8,128)S(1)}, s32[4,32]{1,0:T(4,128)S(1)}, pred[4,32]{1,0:T(4,128)(4,1)S(1)}, bf16[4,32,128,128]{3,2,1,0:T(8,...) while((s32[]{:T(128)}, f32[4,128,512]{2,1,0:T(8,128)S(1)}, ...), condition=%wide.region_2.3_spmd, body=%wide.region_0.2_spmd.sunk | while | flops 543164928 | bytes 47196676 | solution.py:34
  36.3 1.4 gather_fusion
  37.7 4.0 %gather_fusion.1 = bf16[32,128,512]{2,1,0:T(8,128)(2,1)} fusion(bf16[8,128,512]{2,1,0:T(8,128)(2,1)} %get-tuple-element.141, s32[1024]{0:T(1024)S(1)} %pad_clamp_fusion.5), kind=kCustom, calls=%fused_computation.1.clone.1 | custom fusion | bytes 8388736 | tf_op jit(solution)/shard_map/while/body/eval_jaxpr/jit(_take)/gather | solution.py:58
  41.7 7.1 %broadcast_select_fusion.2 = f32[32,128,512]{2,1,0:T(8,128)} fusion(pred[32]{0:T(512)(128)(4,1)S(1)} %dynamic-slice_bitcast_fusion.2, bf16[32,128,512]{2,1,0:T(8,128)(2,1)} %gather_fusion.1, pred[32]{0:T(512)(128)(4,1)S(1)} %compare_and_fusion.2, bf16[4,32,128,128]{3,2,1,0:T(8,128)(2,1)} %get-tuple-element.138, s32[]{:T(128)} %get-tuple-element.125), kind=kOutput, calls=%fused_computation.3.clone.1 | convolution fusion | flops 541065216 | bytes 13632064 | tf_op jit(solution)/shard_map/while/body/eval_jaxpr/gij,gjf->gif/dot_general | solution.py:28
  48.8 11.7 %scatter_fusion = f32[4,128,512]{2,1,0:T(8,128)S(1)} fusion(f32[4,128,512]{2,1,0:T(8,128)S(1)} %get-tuple-element.126, s32[32]{0:T(128)S(1)} %get-tuple-element.114, f32[32,128,512]{2,1,0:T(8,128)} %broadcast_select_fusion.2), kind=kCustom, calls=%fused_computation.2.clone.1 | custom fusion | flops 2097152 | bytes 25165952 | tf_op jit(solution)/shard_map/while/body/eval_jaxpr/scatter-add | solution.py:32
  60.5 1.4 gather_fusion
  61.9 4.0 %gather_fusion.1 = bf16[32,128,512]{2,1,0:T(8,128)(2,1)} fusion(bf16[8,128,512]{2,1,0:T(8,128)(2,1)} %get-tuple-element.141, s32[1024]{0:T(1024)S(1)} %pad_clamp_fusion.5), kind=kCustom, calls=%fused_computation.1.clone.1 | custom fusion | bytes 8388736 | tf_op jit(solution)/shard_map/while/body/eval_jaxpr/jit(_take)/gather | solution.py:58
  65.9 7.1 %broadcast_select_fusion.2 = f32[32,128,512]{2,1,0:T(8,128)} fusion(pred[32]{0:T(512)(128)(4,1)S(1)} %dynamic-slice_bitcast_fusion.2, bf16[32,128,512]{2,1,0:T(8,128)(2,1)} %gather_fusion.1, pred[32]{0:T(512)(128)(4,1)S(1)} %compare_and_fusion.2, bf16[4,32,128,128]{3,2,1,0:T(8,128)(2,1)} %get-tuple-element.138, s32[]{:T(128)} %get-tuple-element.125), kind=kOutput, calls=%fused_computation.3.clone.1 | convolution fusion | flops 541065216 | bytes 13632064 | tf_op jit(solution)/shard_map/while/body/eval_jaxpr/gij,gjf->gif/dot_general | solution.py:28
  73.0 11.7 %scatter_fusion = f32[4,128,512]{2,1,0:T(8,128)S(1)} fusion(f32[4,128,512]{2,1,0:T(8,128)S(1)} %get-tuple-element.126, s32[32]{0:T(128)S(1)} %get-tuple-element.114, f32[32,128,512]{2,1,0:T(8,128)} %broadcast_select_fusion.2), kind=kCustom, calls=%fused_computation.2.clone.1 | custom fusion | flops 2097152 | bytes 25165952 | tf_op jit(solution)/shard_map/while/body/eval_jaxpr/scatter-add | solution.py:32
  84.7 1.4 gather_fusion
  86.1 4.0 %gather_fusion.1 = bf16[32,128,512]{2,1,0:T(8,128)(2,1)} fusion(bf16[8,128,512]{2,1,0:T(8,128)(2,1)} %get-tuple-element.141, s32[1024]{0:T(1024)S(1)} %pad_clamp_fusion.5), kind=kCustom, calls=%fused_computation.1.clone.1 | custom fusion | bytes 8388736 | tf_op jit(solution)/shard_map/while/body/eval_jaxpr/jit(_take)/gather | solution.py:58
  90.1 7.1 %broadcast_select_fusion.2 = f32[32,128,512]{2,1,0:T(8,128)} fusion(pred[32]{0:T(512)(128)(4,1)S(1)} %dynamic-slice_bitcast_fusion.2, bf16[32,128,512]{2,1,0:T(8,128)(2,1)} %gather_fusion.1, pred[32]{0:T(512)(128)(4,1)S(1)} %compare_and_fusion.2, bf16[4,32,128,128]{3,2,1,0:T(8,128)(2,1)} %get-tuple-element.138, s32[]{:T(128)} %get-tuple-element.125), kind=kOutput, calls=%fused_computation.3.clone.1 | convolution fusion | flops 541065216 | bytes 13632064 | tf_op jit(solution)/shard_map/while/body/eval_jaxpr/gij,gjf->gif/dot_general | solution.py:28
  97.1 11.7 %scatter_fusion = f32[4,128,512]{2,1,0:T(8,128)S(1)} fusion(f32[4,128,512]{2,1,0:T(8,128)S(1)} %get-tuple-element.126, s32[32]{0:T(128)S(1)} %get-tuple-element.114, f32[32,128,512]{2,1,0:T(8,128)} %broadcast_select_fusion.2), kind=kCustom, calls=%fused_computation.2.clone.1 | custom fusion | flops 2097152 | bytes 25165952 | tf_op jit(solution)/shard_map/while/body/eval_jaxpr/scatter-add | solution.py:32
  108.9 1.4 gather_fusion
  110.2 4.0 %gather_fusion.1 = bf16[32,128,512]{2,1,0:T(8,128)(2,1)} fusion(bf16[8,128,512]{2,1,0:T(8,128)(2,1)} %get-tuple-element.141, s32[1024]{0:T(1024)S(1)} %pad_clamp_fusion.5), kind=kCustom, calls=%fused_computation.1.clone.1 | custom fusion | bytes 8388736 | tf_op jit(solution)/shard_map/while/body/eval_jaxpr/jit(_take)/gather | solution.py:58
  114.3 7.1 %broadcast_select_fusion.2 = f32[32,128,512]{2,1,0:T(8,128)} fusion(pred[32]{0:T(512)(128)(4,1)S(1)} %dynamic-slice_bitcast_fusion.2, bf16[32,128,512]{2,1,0:T(8,128)(2,1)} %gather_fusion.1, pred[32]{0:T(512)(128)(4,1)S(1)} %compare_and_fusion.2, bf16[4,32,128,128]{3,2,1,0:T(8,128)(2,1)} %get-tuple-element.138, s32[]{:T(128)} %get-tuple-element.125), kind=kOutput, calls=%fused_computation.3.clone.1 | convolution fusion | flops 541065216 | bytes 13632064 | tf_op jit(solution)/shard_map/while/body/eval_jaxpr/gij,gjf->gif/dot_general | solution.py:28
  121.3 11.7 %scatter_fusion = f32[4,128,512]{2,1,0:T(8,128)S(1)} fusion(f32[4,128,512]{2,1,0:T(8,128)S(1)} %get-tuple-element.126, s32[32]{0:T(128)S(1)} %get-tuple-element.114, f32[32,128,512]{2,1,0:T(8,128)} %broadcast_select_fusion.2), kind=kCustom, calls=%fused_computation.2.clone.1 | custom fusion | flops 2097152 | bytes 25165952 | tf_op jit(solution)/shard_map/while/body/eval_jaxpr/scatter-add | solution.py:32
  133.0 0.9 convert_element_type.9
  133.9 0.0 reduce-scatter.2.cloned.1.call-update
  133.9 21.7 %reduce-scatter.2.cloned.1.call-done = bf16[128,512]{1,0:T(8,128)(2,1)} async-done(((bf16[512,512]{1,0:T(8,128)(2,1)}), bf16[128,512]{1,0:T(8,128)(2,1)}) %reduce-scatter.2.cloned.1.call-update) | async-done | bytes 131088 | tf_op jit(solution)/shard_map/reduce_scatter | solution.py:62
  155.6 0.0 copy-done
  155.6 2.0 %convolution_convert_fusion = bf16[128,1536]{1,0:T(8,128)(2,1)} fusion(bf16[128,512]{1,0:T(8,128)(2,1)} %reduce-scatter.2.cloned.1.call-done, bf16[512,1536]{1,0:T(8,128)(2,1)S(1)} %copy-done), kind=kOutput, calls=%fused_computation.27 | convolution fusion | flops 201523200 | bytes 2097152 | tf_op jit(solution)/shard_map/dot_general | solution.py:65
  (26 shorter events, 0.2 us)
Async XLA Ops:
  7.2 148.5 %copy-start = (bf16[512,1536]{1,0:T(8,128)(2,1)S(1)}, bf16[512,1536]{1,0:T(8,128)(2,1)}, u32[]{:S(2)}) copy-start(bf16[512,1536]{1,0:T(8,128)(2,1)} %param.13) | copy-start | bytes 4718596
  7.2 28.9 %all-gather.2.cloned.1.call-start = ((), (), s32[]{:S(2)}) async-start(), calls=%async_computation.1 | async-start | bytes 1179648 | tf_op jit(solution)/shard_map/all_gather | solution.py:54
  7.9 147.7 %reduce-scatter.2.cloned.1.call-start = ((), (), s32[]{:S(2)}) async-start(), calls=%async_computation.2 | async-start | bytes 655360 | tf_op jit(solution)/shard_map/reduce_scatter | solution.py:62
Sparse Core Ops, SparseCore 0:
  9.9 26.1 all-gather.1
  134.0 21.5 reduce-scatter.1
where the time goes:
time: 165 us; the launch traced here: 164 us
  other arithmetic  49 us (30%)
  waiting for transfers between devices  48 us (29%)
  matrix products  30.2 us (18%)
  local copies, waits for them, and re-layouts  22.2 us (13%)
  between operations  14.7 us (9%)
    scatter-add x4, other arithmetic, one_group(): return (partial_value.at[rows_now].add(products), None)  46.7 us
    dot_general x4, matrix products, one_group(): jnp.einsum('gij,gjf->gif', blocks_now, block_feats, preferred_element_typ...  28.2 us
    all_gather x1, waiting for transfers between devices, body(): gathered = lax.all_gather(features, 'row', axis=0, tiled=True)  25.6 us
    reduce_scatter x1, waiting for transfers between devices, body(): lax.psum_scatter(partial_rows.astype(jnp.bfloat16), 'col', scatter_dimens...  21.7 us
    gather x8, local copies, waits for them, and re-layouts, feats_whole(): return jnp.take(panel_blocks, col_ids[index_now], axis=0)  21.5 us
  transfers between devices with their start and end apart: 2, of which 2 were waited for; matrix products, arithmetic and copies ran while one was open for 1% of the time, Pallas kernels for 0%

commit v1 on v0

v1 whole, which is shorter than its diff:
```python
import functools

import jax
import jax.numpy as jnp
from jax import lax
from jax.experimental import pallas as pl
from jax.experimental.pallas import tpu as pltpu
from jax.sharding import PartitionSpec as P

MESH = pl.DeviceIdType.MESH
CHUNK = 128
UNROLL = 4


def fused_kernel(
    n_col, feats, adj, rows, cols, count, w, agg, qkv,
    adj_v, prefix, dense, panel, part, got, w_v, meta_v, meta_s,
    local_sem, gather_send, gather_recv, relay_send, sum_send, sum_recv,
):
    slots, side = adj_v.shape[0], adj_v.shape[1]
    n_chunk, n_row = panel.shape[0], panel.shape[1]
    width = panel.shape[3]
    row, col = lax.axis_index("row"), lax.axis_index("col")
    chip_y, chip_x, core = row // 4, (row // 2) % 2, row % 2

    def partner(code):
        y = 1 - chip_y if code & 4 else chip_y
        x = 1 - chip_x if code & 2 else chip_x
        k = 1 - core if code & 1 else core
        return (y * 2 + x) * 2 + k

    adj_copy = pltpu.make_async_copy(adj, adj_v, local_sem.at[0])
    adj_copy.start()
    w_copy = pltpu.make_async_copy(w, w_v, local_sem.at[1])
    w_copy.start()

    barrier = pltpu.get_barrier_semaphore()
    for code in (1, 2, 4, 6):
        pl.semaphore_signal(barrier, inc=1, device_id={"row": partner(code)}, device_id_type=MESH)
    for step in range(1, n_col):
        pl.semaphore_signal(
            barrier, inc=1, device_id={"col": lax.rem(col + step, n_col)}, device_id_type=MESH
        )

    lane = lax.broadcasted_iota(jnp.int32, (slots, slots), 1)
    sub = lax.broadcasted_iota(jnp.int32, (slots, slots), 0)
    coords = (dense.shape[0] // side) * n_row
    key = rows[...] * n_row + cols[...]
    key_lane = jnp.where(lane < count[0, 0], jnp.broadcast_to(key, (slots, slots)), coords)
    key_sub = jnp.transpose(key_lane)
    same_before = jnp.sum(
        ((key_lane == key_sub) & (lane < sub)).astype(jnp.int32), axis=1, keepdims=True
    )
    less = jnp.sum((key_lane < key_sub).astype(jnp.int32), axis=1, keepdims=True)
    placed = (less + same_before) == lane
    order = jnp.sum(jnp.where(placed, sub, 0), axis=0, keepdims=True)
    keep = jnp.sum(
        jnp.where(placed & (same_before > 0), 1, 0), axis=0, keepdims=True
    )
    upto = jnp.sum((key_sub <= lane).astype(jnp.int32), axis=0, keepdims=True)
    here = jnp.sum((key_sub == lane).astype(jnp.int32), axis=0, keepdims=True)
    last = jnp.where(here > 0, upto - 1, slots)
    meta_v[0:1, :] = order
    meta_v[1:2, :] = keep
    meta_v[2:3, :] = last
    meta_v[3:8, :] = jnp.zeros((5, slots), jnp.int32)
    meta_copy = pltpu.make_async_copy(meta_v, meta_s, local_sem.at[2])
    meta_copy.start()

    panel_own = [feats.at[:, pl.ds(ch * width, width)] for ch in range(n_chunk)]
    pl.semaphore_wait(barrier, 4 + n_col - 1)

    sends = []
    for ch in range(n_chunk):
        for slot, code in enumerate((6, 2, 4, 1)):
            copy = pltpu.make_async_remote_copy(
                src_ref=panel_own[ch],
                dst_ref=panel.at[ch, row],
                send_sem=gather_send.at[ch, slot],
                recv_sem=gather_recv.at[ch, code],
                device_id={"row": partner(code)},
                device_id_type=MESH,
            )
            copy.start()
            sends.append(copy)

    for ch in range(n_chunk):
        panel[ch, row] = feats[:, ch * width:(ch + 1) * width]
    prefix[slots] = jnp.zeros((side, side), prefix.dtype)
    meta_copy.wait()
    adj_copy.wait()

    def add_slots(group, running):
        for inner in range(UNROLL):
            at = group * UNROLL + inner
            held = meta_s[1, at].astype(jnp.float32)
            running = running * held + adj_v[meta_s[0, at]].astype(jnp.float32)
            prefix[at] = running.astype(prefix.dtype)
        return running

    lax.fori_loop(0, slots // UNROLL, add_slots, jnp.zeros((side, side), jnp.float32))
    for block_row in range(dense.shape[0] // side):
        for block_col in range(n_row):
            dense[
                block_row * side:(block_row + 1) * side,
                block_col * side:(block_col + 1) * side,
            ] = prefix[meta_s[2, block_row * n_row + block_col]]

    def arrival(ch, code):
        return pltpu.make_async_remote_copy(
            src_ref=panel_own[ch],
            dst_ref=panel.at[ch, partner(code)],
            send_sem=gather_send.at[ch, 0],
            recv_sem=gather_recv.at[ch, code],
            device_id={"row": partner(1)},
            device_id_type=MESH,
        )

    def relay(ch):
        for slot, code in enumerate((2, 4, 6)):
            arrival(ch, code).wait_recv()
            copy = pltpu.make_async_remote_copy(
                src_ref=panel.at[ch, partner(code)],
                dst_ref=panel.at[ch, partner(code)],
                send_sem=relay_send.at[ch, slot],
                recv_sem=gather_recv.at[ch, code + 1],
                device_id={"row": partner(1)},
                device_id_type=MESH,
            )
            copy.start()
            sends.append(copy)

    summed = []
    relay(0)
    for ch in range(n_chunk):
        if ch + 1 < n_chunk:
            relay(ch + 1)
        for code in (1, 3, 5, 7):
            arrival(ch, code).wait_recv()
        product = jnp.dot(
            dense[...],
            panel[ch].reshape(n_row * side, width),
            preferred_element_type=jnp.float32,
        )
        part[ch] = product.reshape(n_col, side, width).astype(part.dtype)
        now = []
        for step in range(n_col - 1, 0, -1):
            to = lax.rem(col + step, n_col)
            copy = pltpu.make_async_remote_copy(
                src_ref=part.at[ch, to],
                dst_ref=got.at[ch, step - 1],
                send_sem=sum_send.at[ch, step - 1],
                recv_sem=sum_recv.at[ch, step - 1],
                device_id={"col": to},
                device_id_type=MESH,
            )
            copy.start()
            now.append(copy)
        summed.append(now)

    w_copy.wait()
    for ch in range(n_chunk):
        total = part[ch, col].astype(jnp.float32)
        for copy in summed[ch]:
            copy.wait_recv()
        for step in range(n_col - 1):
            total = total + got[ch, step].astype(jnp.float32)
        agg[:, ch * width:(ch + 1) * width] = total.astype(agg.dtype)
    qkv[...] = jnp.dot(agg[...], w_v[...], preferred_element_type=jnp.float32).astype(qkv.dtype)
    for now in summed:
        for copy in now:
            copy.wait_send()
    for copy in sends:
        copy.wait_send()


def fused_body(n_row, n_col, features, adj_blocks, block_rows, block_cols, block_counts, w_qkv):
    cells, feat_width = features.shape[0], features.shape[2]
    slots, side = adj_blocks.shape[2], adj_blocks.shape[3]
    out_width = w_qkv.shape[1]
    n_chunk = feat_width // CHUNK
    vmem = pl.BlockSpec(memory_space=pltpu.VMEM)
    hbm = pl.BlockSpec(memory_space=pl.ANY)
    dma = pltpu.SemaphoreType.DMA
    kind = features.dtype
    return pl.pallas_call(
        functools.partial(fused_kernel, n_col),
        out_shape=(
            jax.ShapeDtypeStruct((cells, feat_width), kind),
            jax.ShapeDtypeStruct((cells, out_width), kind),
        ),
        in_specs=[vmem, hbm, vmem, vmem, pl.BlockSpec(memory_space=pltpu.SMEM), hbm],
        out_specs=(vmem, vmem),
        scratch_shapes=[
            pltpu.VMEM((slots, side, side), kind),
            pltpu.VMEM((slots + 1, side, side), kind),
            pltpu.VMEM((n_col * side, n_row * side), kind),
            pltpu.VMEM((n_chunk, n_row, side, CHUNK), kind),
            pltpu.VMEM((n_chunk, n_col, side, CHUNK), kind),
            pltpu.VMEM((n_chunk, n_col - 1, side, CHUNK), kind),
            pltpu.VMEM(w_qkv.shape, kind),
            pltpu.VMEM((8, slots), jnp.int32),
            pltpu.SMEM((8, slots), jnp.int32),
            dma((3,)),
            dma((n_chunk, 4)),
            dma((n_chunk, 8)),
            dma((n_chunk, 3)),
            dma((n_chunk, n_col - 1)),
            dma((n_chunk, n_col - 1)),
        ],
        compiler_params=pltpu.CompilerParams(
            collective_id=0, has_side_effects=True, vmem_limit_bytes=48 << 20
        ),
    )(
        features[:, 0, :], adj_blocks[0, 0], block_rows[0], block_cols[0], block_counts, w_qkv
    )


def general_body(features, adj_blocks, block_rows, block_cols, block_counts, w_qkv):
    tile_blocks, row_ids, col_ids = adj_blocks[0, 0], block_rows[0, 0], block_cols[0, 0]
    side, feat_width = tile_blocks.shape[1], features.shape[2]
    slots = tile_blocks.shape[0]
    group = 32
    tile_cells = features.shape[0] * lax.axis_size("col")
    live = jnp.arange(slots, dtype=jnp.int32) < block_counts[0, 0]
    gathered = lax.all_gather(features, "row", axis=0, tiled=True)
    panel = gathered[:, 0, :].reshape(-1, side, feat_width)

    def one_group(partial_value, inputs):
        blocks_now, rows_now, cols_now, live_now = inputs
        products = jnp.einsum(
            "gij,gjf->gif", blocks_now, jnp.take(panel, cols_now, axis=0),
            preferred_element_type=jnp.float32,
        )
        products = jnp.where(live_now[:, None, None], products, jnp.float32(0.0))
        return partial_value.at[rows_now].add(products), None

    start = jnp.zeros((tile_cells // side, side, feat_width), jnp.float32)
    partial_value, _ = lax.scan(
        one_group, start,
        (
            tile_blocks.reshape(-1, group, side, side),
            row_ids.reshape(-1, group), col_ids.reshape(-1, group), live.reshape(-1, group),
        ),
    )
    summed = lax.psum_scatter(
        partial_value.reshape(tile_cells, feat_width).astype(jnp.bfloat16),
        "col", scatter_dimension=0, tiled=True,
    )
    qkv = jnp.dot(summed, w_qkv, preferred_element_type=jnp.float32).astype(jnp.bfloat16)
    return summed, qkv


def solution(mesh):
    n_row, n_col = mesh.shape["row"], mesh.shape["col"]
    body = functools.partial(fused_body, n_row, n_col) if n_row == 8 and n_col <= 8 else general_body
    placed = (
        P("row", "col", None),
        P("row", "col", None, None, None),
        P("row", "col", None),
        P("row", "col", None),
        P("row", "col"),
        P(),
    )
    return jax.shard_map(
        body,
        mesh=mesh,
        in_specs=placed,
        out_specs=(P(("row", "col"), None), P(("row", "col"), None)),
        check_vma=False,
    )
```

time: 165 us -> 32.5 us (0.20)
  other arithmetic: 49 us -> 0 us
  waiting for transfers between devices: 48 us -> 0 us
  matrix products: 30.2 us -> 0 us
  Pallas kernels: 0 us -> 25.9 us
  local copies, waits for them, and re-layouts: 22.2 us -> 5.02 us
  between operations: 14.7 us -> 1.3 us
    scatter-add x4 -> x0, other arithmetic: 46.7 us -> none  [one_group(): return (partial_value.at[rows_now].add(products), None)]
    dot_general x5 -> x0, matrix products: 30.2 us -> none  [the longest x4 28.2 us: one_group(): jnp.einsum('gij,gjf->gif', blocks_now, block_feats, preferred_element_typ...]
    pallas_call x0 -> x1, Pallas kernels: none -> 25.9 us  [fused_body(): pl.pallas_call(functools.partial(fused_kernel, n_col), out_shape=(jax.Sha...]
    all_gather x1 -> x0, waiting for transfers between devices: 25.6 us -> none  [body(): gathered = lax.all_gather(features, 'row', axis=0, tiled=True)]
    reduce_scatter x1 -> x0, waiting for transfers between devices: 21.7 us -> none  [body(): lax.psum_scatter(partial_rows.astype(jnp.bfloat16), 'col', scatter_dimens...]
    gather x8 -> x0, local copies, waits for them, and re-layouts: 21.5 us -> none  [feats_whole(): return jnp.take(panel_blocks, col_ids[index_now], axis=0)]
    unnamed x3 -> x10, local copies, waits for them, and re-layouts: 0.52 us -> 5.02 us
  transfers between devices with their start and end apart: 2 -> 0, of which waited for: 2 -> 0; matrix products, arithmetic and copies ran while one was open for 1% -> 0% of each run, Pallas kernels for 0% -> 0%
where the time goes in v1:
time: 32.5 us; the launch traced here: 32.3 us
  Pallas kernels  25.9 us (80%)
  local copies, waits for them, and re-layouts  5.02 us (15%)
  between operations  1.3 us (4%)
    pallas_call x1, Pallas kernels, fused_body(): pl.pallas_call(functools.partial(fused_kernel, n_col), out_shape=(jax.Sha...  25.9 us
    unnamed x10, local copies, waits for them, and re-layouts  5.02 us

profile of v1, /device:TPU:0, one launch (start us, length us, event | category | flops | bytes accessed | tf_op | source)
XLA Modules:
  0.0 32.3 jit_solution(4423047372645767739)
XLA Ops:
  1.3 0.0 copy-start
  1.3 1.4 %copy-done = bf16[512,1536]{1,0:T(8,128)(2,1)S(1)} copy-done((bf16[512,1536]{1,0:T(8,128)(2,1)S(1)}, bf16[512,1536]{1,0:T(8,128)(2,1)}, u32[]{:S(2)}) %copy-start) | copy-done | bytes 1572888
  2.7 0.0 copy-start.1
  2.7 0.9 %copy-done.1 = bf16[128,1,512]{2,0,1:T(8,128)(2,1)S(1)} copy-done((bf16[128,1,512]{2,0,1:T(8,128)(2,1)S(1)}, bf16[128,1,512]{2,0,1:T(8,128)(2,1)}, u32[]{:S(2)}) %copy-start.1) | copy-done | bytes 131096
  3.6 0.0 copy-start.2
  3.6 0.7 %copy-done.2 = s32[1,1,128]{2,1,0:T(1,128)S(1)} copy-done((s32[1,1,128]{2,1,0:T(1,128)S(1)}, s32[1,1,128]{2,1,0:T(1,128)}, u32[]{:S(2)}) %copy-start.2) | copy-done | bytes 536
  4.2 0.0 copy-start.3
  4.2 0.7 %copy-done.3 = s32[1,1,128]{2,1,0:T(1,128)S(1)} copy-done((s32[1,1,128]{2,1,0:T(1,128)S(1)}, s32[1,1,128]{2,1,0:T(1,128)}, u32[]{:S(2)}) %copy-start.3) | copy-done | bytes 536
  4.9 25.9 %shard_map.77 = (bf16[128,512]{1,0:T(8,128)(2,1)S(1)}, bf16[128,1536]{1,0:T(8,128)(2,1)S(1)}) custom-call(bf16[128,512]{1,0:T(8,128)(2,1)S(1)} %bitcast.4, bf16[128,128,128]{2,1,0:T(8,128)(2,1)} %bitcast.7, s32[1,128]{1,0:T(1,128)S(1)} %bitcast.5, s32[1,128]{1,0:T(1,128)S(1)} %bitcast.6, s32[1,1]{1,0:T(1,128)S(6)} %copy.10.count, bf16[512,1536]{1,0:T(8,128)(2,1)S(1)} %copy-done), custom_call_target="tpu_custom_call" | custom-call | tf_op jit(solution)/shard_map/pallas_call | solution.py:186
  30.9 0.7 %copy.11 = bf16[128,512]{1,0:T(8,128)(2,1)} copy(bf16[128,512]{1,0:T(8,128)(2,1)S(1)} %get-tuple-element.4) | data formatting | bytes 262144
  31.5 0.7 %copy.12 = bf16[128,1536]{1,0:T(8,128)(2,1)} copy(bf16[128,1536]{1,0:T(8,128)(2,1)S(1)} %get-tuple-element.5) | data formatting | bytes 786432
Async XLA Ops:
  1.3 1.4 %copy-start = (bf16[512,1536]{1,0:T(8,128)(2,1)S(1)}, bf16[512,1536]{1,0:T(8,128)(2,1)}, u32[]{:S(2)}) copy-start(bf16[512,1536]{1,0:T(8,128)(2,1)} %w.1) | copy-start | bytes 4718596
  2.7 0.9 %copy-start.1 = (bf16[128,1,512]{2,0,1:T(8,128)(2,1)S(1)}, bf16[128,1,512]{2,0,1:T(8,128)(2,1)}, u32[]{:S(2)}) copy-start(bf16[128,1,512]{2,0,1:T(8,128)(2,1)} %param.6) | copy-start | bytes 393220
  3.6 0.7 %copy-start.2 = (s32[1,1,128]{2,1,0:T(1,128)S(1)}, s32[1,1,128]{2,1,0:T(1,128)}, u32[]{:S(2)}) copy-start(s32[1,1,128]{2,1,0:T(1,128)} %param.8) | copy-start | bytes 1540
  4.2 0.7 %copy-start.3 = (s32[1,1,128]{2,1,0:T(1,128)S(1)}, s32[1,1,128]{2,1,0:T(1,128)}, u32[]{:S(2)}) copy-start(s32[1,1,128]{2,1,0:T(1,128)} %param.9) | copy-start | bytes 1540

commit v2 on v1

--- a/solution.py
+++ b/solution.py
@@ -10,11 +10,12 @@
 MESH = pl.DeviceIdType.MESH
 CHUNK = 128
 UNROLL = 4
+AHEAD = 4
 
 
 def fused_kernel(
     n_col, feats, adj, rows, cols, count, w, agg, qkv,
-    adj_v, prefix, dense, panel, part, got, w_v, meta_v, meta_s,
+    adj_v, prefix, dense, panel, part, got, joint, rough, w_v, coords_v, meta_v, meta_s,
     local_sem, gather_send, gather_recv, relay_send, sum_send, sum_recv,
 ):
     slots, side = adj_v.shape[0], adj_v.shape[1]
@@ -29,8 +30,21 @@
         k = 1 - core if code & 1 else core
         return (y * 2 + x) * 2 + k
 
+    coords_copies = [
+        pltpu.make_async_copy(rows, coords_v.at[0:1], local_sem.at[3]),
+        pltpu.make_async_copy(cols, coords_v.at[8:9], local_sem.at[4]),
+    ]
+    for copy in coords_copies:
+        copy.start()
     adj_copy = pltpu.make_async_copy(adj, adj_v, local_sem.at[0])
     adj_copy.start()
+    panel_own = [feats.at[:, pl.ds(ch * width, width)] for ch in range(n_chunk)]
+    own_copies = [
+        pltpu.make_async_copy(panel_own[ch], panel.at[ch, row], local_sem.at[5 + ch])
+        for ch in range(n_chunk)
+    ]
+    for copy in own_copies:
+        copy.start()
     w_copy = pltpu.make_async_copy(w, w_v, local_sem.at[1])
     w_copy.start()
 
@@ -45,7 +59,9 @@
     lane = lax.broadcasted_iota(jnp.int32, (slots, slots), 1)
     sub = lax.broadcasted_iota(jnp.int32, (slots, slots), 0)
     coords = (dense.shape[0] // side) * n_row
-    key = rows[...] * n_row + cols[...]
+    for copy in coords_copies:
+        copy.wait()
+    key = coords_v[0:1, :] * n_row + coords_v[8:9, :]
     key_lane = jnp.where(lane < count[0, 0], jnp.broadcast_to(key, (slots, slots)), coords)
     key_sub = jnp.transpose(key_lane)
     same_before = jnp.sum(
@@ -67,11 +83,11 @@
     meta_copy = pltpu.make_async_copy(meta_v, meta_s, local_sem.at[2])
     meta_copy.start()
 
-    panel_own = [feats.at[:, pl.ds(ch * width, width)] for ch in range(n_chunk)]
     pl.semaphore_wait(barrier, 4 + n_col - 1)
 
     sends = []
-    for ch in range(n_chunk):
+
+    def send_own(ch):
         for slot, code in enumerate((6, 2, 4, 1)):
             copy = pltpu.make_async_remote_copy(
                 src_ref=panel_own[ch],
@@ -84,8 +100,8 @@
             copy.start()
             sends.append(copy)
 
-    for ch in range(n_chunk):
-        panel[ch, row] = feats[:, ch * width:(ch + 1) * width]
+    for ch in range(min(AHEAD, n_chunk)):
+        send_own(ch)
     prefix[slots] = jnp.zeros((side, side), prefix.dtype)
     meta_copy.wait()
     adj_copy.wait()
@@ -130,46 +146,99 @@
             copy.start()
             sends.append(copy)
 
-    summed = []
+    at_end = (col == 0) | (col == n_col - 1)
+    upper = col // 2
+
+    def along(place):
+        return place + upper * (n_col - 1 - 2 * place)
+
+    def sum_copy(ch, source, slot, place, sem):
+        return pltpu.make_async_remote_copy(
+            src_ref=source,
+            dst_ref=got.at[ch, slot],
+            send_sem=sum_send.at[ch, sem],
+            recv_sem=sum_recv.at[ch, slot],
+            device_id={"col": along(place)},
+            device_id_type=MESH,
+        )
+
+    def arrived(ch, slot):
+        sum_copy(ch, part.at[ch, 0], slot, 2, 0).wait_recv()
+
+    def send_parts(ch):
+        @pl.when(at_end)
+        def _():
+            sum_copy(ch, part.at[ch, along(3)], 3, 1, 0).start()
+            sum_copy(ch, part.at[ch, along(2)], 2, 2, 1).start()
+            sum_copy(ch, part.at[ch, along(1)], 0, 1, 2).start()
+
+        @pl.when(jnp.logical_not(at_end))
+        def _():
+            sum_copy(ch, part.at[ch, along(2)], 1, 2, 1).start()
+            sum_copy(ch, part.at[ch, along(0)], 0, 0, 2).start()
+
+    def pass_on(ch):
+        @pl.when(jnp.logical_not(at_end))
+        def _():
+            arrived(ch, 3)
+            both = part[ch, along(3)].astype(jnp.float32) + got[ch, 3].astype(jnp.float32)
+            joint[ch] = both.astype(joint.dtype)
+            sum_copy(ch, joint.at[ch], 1, 3, 0).start()
+
+    def finish(ch):
+        lanes = slice(ch * width, (ch + 1) * width)
+        for slot in (0, 1):
+            arrived(ch, slot)
+        total = part[ch, col].astype(jnp.float32)
+        total = total + got[ch, 0].astype(jnp.float32) + got[ch, 1].astype(jnp.float32)
+
+        @pl.when(at_end)
+        def _():
+            agg[:, lanes] = total.astype(agg.dtype)
+
+        @pl.when(jnp.logical_not(at_end))
+        def _():
+            arrived(ch, 2)
+            agg[:, lanes] = (total + got[ch, 2].astype(jnp.float32)).astype(agg.dtype)
+
     relay(0)
     for ch in range(n_chunk):
+        if ch + AHEAD < n_chunk:
+            send_own(ch + AHEAD)
         if ch + 1 < n_chunk:
             relay(ch + 1)
         for code in (1, 3, 5, 7):
             arrival(ch, code).wait_recv()
+        own_copies[ch].wait()
         product = jnp.dot(
             dense[...],
             panel[ch].reshape(n_row * side, width),
             preferred_element_type=jnp.float32,
         )
         part[ch] = product.reshape(n_col, side, width).astype(part.dtype)
-        now = []
-        for step in range(n_col - 1, 0, -1):
-            to = lax.rem(col + step, n_col)
-            copy = pltpu.make_async_remote_copy(
-                src_ref=part.at[ch, to],
-                dst_ref=got.at[ch, step - 1],
-                send_sem=sum_send.at[ch, step - 1],
-                recv_sem=sum_recv.at[ch, step - 1],
-                device_id={"col": to},
-                device_id_type=MESH,
-            )
-            copy.start()
-            now.append(copy)
-        summed.append(now)
+        send_parts(ch)
+        if ch >= 1:
+            pass_on(ch - 1)
+    pass_on(n_chunk - 1)
 
     w_copy.wait()
+    for ch in range(n_chunk - 1):
+        finish(ch)
+    early = (n_chunk - 1) * width
+    for at in range(0, qkv.shape[1], 512):
+        rows_early = jnp.dot(
+            agg[:, :early], w_v[:early, at:at + 512], preferred_element_type=jnp.float32
+        )
+        rough[:, at:at + 512] = rows_early
+    finish(n_chunk - 1)
+    for at in range(0, qkv.shape[1], 512):
+        rows_late = jnp.dot(
+            agg[:, early:], w_v[early:, at:at + 512], preferred_element_type=jnp.float32
+        )
+        qkv[:, at:at + 512] = (rough[:, at:at + 512] + rows_late).astype(qkv.dtype)
     for ch in range(n_chunk):
-        total = part[ch, col].astype(jnp.float32)
-        for copy in summed[ch]:
-            copy.wait_recv()
-        for step in range(n_col - 1):
-            total = total + got[ch, step].astype(jnp.float32)
-        agg[:, ch * width:(ch + 1) * width] = total.astype(agg.dtype)
-    qkv[...] = jnp.dot(agg[...], w_v[...], preferred_element_type=jnp.float32).astype(qkv.dtype)
-    for now in summed:
-        for copy in now:
-            copy.wait_send()
+        for sem in range(3):
+            sum_copy(ch, part.at[ch, 0], 0, 2, sem).wait_send()
     for copy in sends:
         copy.wait_send()
 
@@ -180,7 +249,7 @@
     out_width = w_qkv.shape[1]
     n_chunk = feat_width // CHUNK
     vmem = pl.BlockSpec(memory_space=pltpu.VMEM)
-    hbm = pl.BlockSpec(memory_space=pl.ANY)
+    hbm = pl.BlockSpec(memory_space=pltpu.MemorySpace.HBM)
     dma = pltpu.SemaphoreType.DMA
     kind = features.dtype
     return pl.pallas_call(
@@ -189,7 +258,7 @@
             jax.ShapeDtypeStruct((cells, feat_width), kind),
             jax.ShapeDtypeStruct((cells, out_width), kind),
         ),
-        in_specs=[vmem, hbm, vmem, vmem, pl.BlockSpec(memory_space=pltpu.SMEM), hbm],
+        in_specs=[hbm, hbm, hbm, hbm, pl.BlockSpec(memory_space=pltpu.SMEM), hbm],
         out_specs=(vmem, vmem),
         scratch_shapes=[
             pltpu.VMEM((slots, side, side), kind),
@@ -197,19 +266,22 @@
             pltpu.VMEM((n_col * side, n_row * side), kind),
             pltpu.VMEM((n_chunk, n_row, side, CHUNK), kind),
             pltpu.VMEM((n_chunk, n_col, side, CHUNK), kind),
-            pltpu.VMEM((n_chunk, n_col - 1, side, CHUNK), kind),
+            pltpu.VMEM((n_chunk, n_col, side, CHUNK), kind),
+            pltpu.VMEM((n_chunk, side, CHUNK), kind),
+            pltpu.VMEM((cells, out_width), jnp.float32),
             pltpu.VMEM(w_qkv.shape, kind),
+            pltpu.VMEM((16, slots), jnp.int32),
             pltpu.VMEM((8, slots), jnp.int32),
             pltpu.SMEM((8, slots), jnp.int32),
-            dma((3,)),
+            dma((5 + n_chunk,)),
             dma((n_chunk, 4)),
             dma((n_chunk, 8)),
             dma((n_chunk, 3)),
-            dma((n_chunk, n_col - 1)),
-            dma((n_chunk, n_col - 1)),
+            dma((n_chunk, 3)),
+            dma((n_chunk, n_col)),
         ],
         compiler_params=pltpu.CompilerParams(
-            collective_id=0, has_side_effects=True, vmem_limit_bytes=48 << 20
+            collective_id=0, has_side_effects=True, vmem_limit_bytes=56 << 20
         ),
     )(
         features[:, 0, :], adj_blocks[0, 0], block_rows[0], block_cols[0], block_counts, w_qkv
@@ -253,7 +325,7 @@
 
 def solution(mesh):
     n_row, n_col = mesh.shape["row"], mesh.shape["col"]
-    body = functools.partial(fused_body, n_row, n_col) if n_row == 8 and n_col <= 8 else general_body
+    body = functools.partial(fused_body, n_row, n_col) if n_row == 8 and n_col == 4 else general_body
     placed = (
         P("row", "col", None),
         P("row", "col", None, None, None),

time: 32.5 us -> 31.1 us (0.957)
  local copies, waits for them, and re-layouts: 5.02 us -> 3.33 us
  Pallas kernels: 25.9 us -> 26.3 us
    unnamed x10 -> x2, local copies, waits for them, and re-layouts: 5.02 us -> 3.33 us
    pallas_call x1, Pallas kernels: 25.9 us -> 26.3 us  [fused_body(): pl.pallas_call(functools.partial(fused_kernel, n_col), out_shape=(jax.Sha...]
where the time goes in v2:
time: 31.1 us; the launch traced here: 31 us
  Pallas kernels  26.3 us (85%)
  local copies, waits for them, and re-layouts  3.33 us (11%)
  between operations  1.29 us (4%)
    pallas_call x1, Pallas kernels, fused_body(): pl.pallas_call(functools.partial(fused_kernel, n_col), out_shape=(jax.Sha...  26.3 us
    unnamed x2, local copies, waits for them, and re-layouts  3.33 us

profile of v2, /device:TPU:0, one launch (start us, length us, event | category | flops | bytes accessed | tf_op | source)
XLA Modules:
  0.0 31.0 jit_solution(605533595548129198)
XLA Ops:
  1.3 26.3 %shard_map.77 = (bf16[128,512]{1,0:T(8,128)(2,1)}, bf16[128,1536]{1,0:T(8,128)(2,1)}) custom-call(bf16[128,512]{1,0:T(8,128)(2,1)} %bitcast.5, bf16[128,128,128]{2,1,0:T(8,128)(2,1)} %bitcast.4, s32[1,128]{1,0:T(1,128)} %bitcast.6, s32[1,128]{1,0:T(1,128)} %bitcast.7, s32[1,1]{1,0:T(1,128)S(6)} %copy.10.count, bf16[512,1536]{1,0:T(8,128)(2,1)} %w.1), custom_call_target="tpu_custom_call" | custom-call | tf_op jit(solution)/shard_map/pallas_call | solution.py:255
  27.6 1.6 %copy.11 = bf16[128,512]{1,0:T(8,128)(2,1)} copy(bf16[128,512]{1,0:T(8,128)(2,1)} %get-tuple-element.4) | data formatting | bytes 262144
  29.2 1.8 %copy.12 = bf16[128,1536]{1,0:T(8,128)(2,1)} copy(bf16[128,1536]{1,0:T(8,128)(2,1)} %get-tuple-element.5) | data formatting | bytes 786432

commit v3 on v2

--- a/solution.py
+++ b/solution.py
@@ -10,12 +10,12 @@
 MESH = pl.DeviceIdType.MESH
 CHUNK = 128
 UNROLL = 4
-AHEAD = 4
+AHEAD = 2
 
 
 def fused_kernel(
-    n_col, feats, adj, rows, cols, count, w, agg, qkv,
-    adj_v, prefix, dense, panel, part, got, joint, rough, w_v, coords_v, meta_v, meta_s,
+    n_col, feats, adj, rows, cols, count, agg,
+    adj_v, prefix, dense, panel, part, got, joint, coords_v, meta_v, meta_s,
     local_sem, gather_send, gather_recv, relay_send, sum_send, sum_recv,
 ):
     slots, side = adj_v.shape[0], adj_v.shape[1]
@@ -45,8 +45,6 @@
     ]
     for copy in own_copies:
         copy.start()
-    w_copy = pltpu.make_async_copy(w, w_v, local_sem.at[1])
-    w_copy.start()
 
     barrier = pltpu.get_barrier_semaphore()
     for code in (1, 2, 4, 6):
@@ -58,7 +56,7 @@
 
     lane = lax.broadcasted_iota(jnp.int32, (slots, slots), 1)
     sub = lax.broadcasted_iota(jnp.int32, (slots, slots), 0)
-    coords = (dense.shape[0] // side) * n_row
+    coords = n_col * n_row
     for copy in coords_copies:
         copy.wait()
     key = coords_v[0:1, :] * n_row + coords_v[8:9, :]
@@ -115,11 +113,13 @@
         return running
 
     lax.fori_loop(0, slots // UNROLL, add_slots, jnp.zeros((side, side), jnp.float32))
-    for block_row in range(dense.shape[0] // side):
+    for block_row in range(n_col):
         for block_col in range(n_row):
+            half = block_col % 2
             dense[
+                block_col // 2,
                 block_row * side:(block_row + 1) * side,
-                block_col * side:(block_col + 1) * side,
+                half * side:(half + 1) * side,
             ] = prefix[meta_s[2, block_row * n_row + block_col]]
 
     def arrival(ch, code):
@@ -205,42 +205,63 @@
     for ch in range(n_chunk):
         if ch + AHEAD < n_chunk:
             send_own(ch + AHEAD)
+        product = None
+        for code in (0, 2, 4, 6):
+            if code == 0:
+                own_copies[ch].wait()
+            arrival(ch, code + 1).wait_recv()
+            pair = partner(code) // 2
+            piece = jnp.dot(
+                dense[pair],
+                panel[ch, pl.ds(pair * 2, 2)].reshape(2 * side, width),
+                preferred_element_type=jnp.float32,
+            )
+            product = piece if product is None else product + piece
+        part[ch] = product.reshape(n_col, side, width).astype(part.dtype)
+        send_parts(ch)
         if ch + 1 < n_chunk:
             relay(ch + 1)
-        for code in (1, 3, 5, 7):
-            arrival(ch, code).wait_recv()
-        own_copies[ch].wait()
-        product = jnp.dot(
-            dense[...],
-            panel[ch].reshape(n_row * side, width),
-            preferred_element_type=jnp.float32,
-        )
-        part[ch] = product.reshape(n_col, side, width).astype(part.dtype)
-        send_parts(ch)
         if ch >= 1:
             pass_on(ch - 1)
     pass_on(n_chunk - 1)
 
-    w_copy.wait()
-    for ch in range(n_chunk - 1):
+    for ch in range(n_chunk):
         finish(ch)
-    early = (n_chunk - 1) * width
-    for at in range(0, qkv.shape[1], 512):
-        rows_early = jnp.dot(
-            agg[:, :early], w_v[:early, at:at + 512], preferred_element_type=jnp.float32
-        )
-        rough[:, at:at + 512] = rows_early
-    finish(n_chunk - 1)
-    for at in range(0, qkv.shape[1], 512):
-        rows_late = jnp.dot(
-            agg[:, early:], w_v[early:, at:at + 512], preferred_element_type=jnp.float32
-        )
-        qkv[:, at:at + 512] = (rough[:, at:at + 512] + rows_late).astype(qkv.dtype)
     for ch in range(n_chunk):
         for sem in range(3):
             sum_copy(ch, part.at[ch, 0], 0, 2, sem).wait_send()
     for copy in sends:
         copy.wait_send()
+
+
+def project_kernel(agg, w, agg_out, qkv, agg_v, w_v, qkv_v, in_sem, out_sem):
+    width = w.shape[1]
+    step = 512 if width % 512 == 0 else width
+    agg_copy = pltpu.make_async_copy(agg, agg_v, in_sem.at[0])
+    agg_copy.start()
+    w_copies = []
+    for at in range(0, width, step):
+        copy = pltpu.make_async_copy(
+            w.at[:, pl.ds(at, step)], w_v.at[:, pl.ds(at, step)], in_sem.at[1 + at // step]
+        )
+        copy.start()
+        w_copies.append(copy)
+    agg_copy.wait()
+    outs = [pltpu.make_async_copy(agg_v, agg_out, out_sem.at[0])]
+    outs[0].start()
+    for at, w_copy in zip(range(0, width, step), w_copies):
+        w_copy.wait()
+        lanes = slice(at, at + step)
+        qkv_v[:, lanes] = jnp.dot(
+            agg_v[...], w_v[:, lanes], preferred_element_type=jnp.float32
+        ).astype(qkv_v.dtype)
+        copy = pltpu.make_async_copy(
+            qkv_v.at[:, pl.ds(at, step)], qkv.at[:, pl.ds(at, step)], out_sem.at[1 + at // step]
+        )
+        copy.start()
+        outs.append(copy)
+    for copy in outs:
+        copy.wait()
 
 
 def fused_body(n_row, n_col, features, adj_blocks, block_rows, block_cols, block_counts, w_qkv):
@@ -252,24 +273,19 @@
     hbm = pl.BlockSpec(memory_space=pltpu.MemorySpace.HBM)
     dma = pltpu.SemaphoreType.DMA
     kind = features.dtype
-    return pl.pallas_call(
+    summed = pl.pallas_call(
         functools.partial(fused_kernel, n_col),
-        out_shape=(
-            jax.ShapeDtypeStruct((cells, feat_width), kind),
-            jax.ShapeDtypeStruct((cells, out_width), kind),
-        ),
-        in_specs=[hbm, hbm, hbm, hbm, pl.BlockSpec(memory_space=pltpu.SMEM), hbm],
-        out_specs=(vmem, vmem),
+        out_shape=jax.ShapeDtypeStruct((cells, feat_width), kind),
+        in_specs=[hbm, hbm, hbm, hbm, pl.BlockSpec(memory_space=pltpu.SMEM)],
+        out_specs=vmem,
         scratch_shapes=[
             pltpu.VMEM((slots, side, side), kind),
             pltpu.VMEM((slots + 1, side, side), kind),
-            pltpu.VMEM((n_col * side, n_row * side), kind),
+            pltpu.VMEM((n_row // 2, n_col * side, 2 * side), kind),
             pltpu.VMEM((n_chunk, n_row, side, CHUNK), kind),
             pltpu.VMEM((n_chunk, n_col, side, CHUNK), kind),
             pltpu.VMEM((n_chunk, n_col, side, CHUNK), kind),
             pltpu.VMEM((n_chunk, side, CHUNK), kind),
-            pltpu.VMEM((cells, out_width), jnp.float32),
-            pltpu.VMEM(w_qkv.shape, kind),
             pltpu.VMEM((16, slots), jnp.int32),
             pltpu.VMEM((8, slots), jnp.int32),
             pltpu.SMEM((8, slots), jnp.int32),
@@ -283,9 +299,24 @@
         compiler_params=pltpu.CompilerParams(
             collective_id=0, has_side_effects=True, vmem_limit_bytes=56 << 20
         ),
-    )(
-        features[:, 0, :], adj_blocks[0, 0], block_rows[0], block_cols[0], block_counts, w_qkv
-    )
+    )(features[:, 0, :], adj_blocks[0, 0], block_rows[0], block_cols[0], block_counts)
+    return pl.pallas_call(
+        project_kernel,
+        out_shape=(
+            jax.ShapeDtypeStruct((cells, feat_width), kind),
+            jax.ShapeDtypeStruct((cells, out_width), kind),
+        ),
+        in_specs=[hbm, hbm],
+        out_specs=(hbm, hbm),
+        scratch_shapes=[
+            pltpu.VMEM((cells, feat_width), kind),
+            pltpu.VMEM(w_qkv.shape, kind),
+            pltpu.VMEM((cells, out_width), kind),
+            dma((1 + max(1, out_width // 512),)),
+            dma((1 + max(1, out_width // 512),)),
+        ],
+        compiler_params=pltpu.CompilerParams(vmem_limit_bytes=56 << 20),
+    )(summed, w_qkv)
 
 
 def general_body(features, adj_blocks, block_rows, block_cols, block_counts, w_qkv):

time: 31.1 us -> 28.6 us (0.920)
  local copies, waits for them, and re-layouts: 3.33 us -> 0 us
  Pallas kernels: 26.3 us -> 27.1 us
    unnamed x2 -> x0, local copies, waits for them, and re-layouts: 3.33 us -> none
    pallas_call x1 -> x2, Pallas kernels: 26.3 us -> 27.1 us  [the longest x1 24.6 us: fused_body(): pl.pallas_call(functools.partial(fused_kernel, n_col), out_shape=jax.Shap...]
where the time goes in v3:
time: 28.6 us; the launch traced here: 28.4 us
  Pallas kernels  27.1 us (95%)
  between operations  1.29 us (5%)
    pallas_call x1, Pallas kernels, fused_body(): pl.pallas_call(functools.partial(fused_kernel, n_col), out_shape=jax.Shap...  24.6 us
    pallas_call x1, Pallas kernels, fused_body(): pl.pallas_call(project_kernel, out_shape=(jax.ShapeDtypeStruct((cells, fe...  2.55 us

profile of v3, /device:TPU:0, one launch (start us, length us, event | category | flops | bytes accessed | tf_op | source)
XLA Modules:
  0.0 28.4 jit_solution(10067762349855476372)
XLA Ops:
  1.3 24.6 %shard_map.77.agg = bf16[128,512]{1,0:T(8,128)(2,1)} custom-call(bf16[128,512]{1,0:T(8,128)(2,1)} %bitcast.5, bf16[128,128,128]{2,1,0:T(8,128)(2,1)} %bitcast.4, s32[1,128]{1,0:T(1,128)} %bitcast.6, s32[1,128]{1,0:T(1,128)} %bitcast.7, s32[1,1]{1,0:T(1,128)S(6)} %copy.8.count), custom_call_target="tpu_custom_call" | custom-call | tf_op jit(solution)/shard_map/pallas_call | solution.py:276
  25.8 2.5 %shard_map.78 = (bf16[128,512]{1,0:T(8,128)(2,1)}, bf16[128,1536]{1,0:T(8,128)(2,1)}) custom-call(bf16[128,512]{1,0:T(8,128)(2,1)} %shard_map.77.agg, bf16[512,1536]{1,0:T(8,128)(2,1)} %w.1), custom_call_target="tpu_custom_call" | custom-call | tf_op jit(solution)/shard_map/pallas_call | solution.py:303

commit v4 on v3

--- a/solution.py
+++ b/solution.py
@@ -9,7 +9,7 @@
 
 MESH = pl.DeviceIdType.MESH
 CHUNK = 128
-UNROLL = 4
+UNROLL = 8
 AHEAD = 2
 
 
@@ -54,33 +54,6 @@
             barrier, inc=1, device_id={"col": lax.rem(col + step, n_col)}, device_id_type=MESH
         )
 
-    lane = lax.broadcasted_iota(jnp.int32, (slots, slots), 1)
-    sub = lax.broadcasted_iota(jnp.int32, (slots, slots), 0)
-    coords = n_col * n_row
-    for copy in coords_copies:
-        copy.wait()
-    key = coords_v[0:1, :] * n_row + coords_v[8:9, :]
-    key_lane = jnp.where(lane < count[0, 0], jnp.broadcast_to(key, (slots, slots)), coords)
-    key_sub = jnp.transpose(key_lane)
-    same_before = jnp.sum(
-        ((key_lane == key_sub) & (lane < sub)).astype(jnp.int32), axis=1, keepdims=True
-    )
-    less = jnp.sum((key_lane < key_sub).astype(jnp.int32), axis=1, keepdims=True)
-    placed = (less + same_before) == lane
-    order = jnp.sum(jnp.where(placed, sub, 0), axis=0, keepdims=True)
-    keep = jnp.sum(
-        jnp.where(placed & (same_before > 0), 1, 0), axis=0, keepdims=True
-    )
-    upto = jnp.sum((key_sub <= lane).astype(jnp.int32), axis=0, keepdims=True)
-    here = jnp.sum((key_sub == lane).astype(jnp.int32), axis=0, keepdims=True)
-    last = jnp.where(here > 0, upto - 1, slots)
-    meta_v[0:1, :] = order
-    meta_v[1:2, :] = keep
-    meta_v[2:3, :] = last
-    meta_v[3:8, :] = jnp.zeros((5, slots), jnp.int32)
-    meta_copy = pltpu.make_async_copy(meta_v, meta_s, local_sem.at[2])
-    meta_copy.start()
-
     pl.semaphore_wait(barrier, 4 + n_col - 1)
 
     sends = []
@@ -100,6 +73,33 @@
 
     for ch in range(min(AHEAD, n_chunk)):
         send_own(ch)
+    lane = lax.broadcasted_iota(jnp.int32, (slots, slots), 1)
+    sub = lax.broadcasted_iota(jnp.int32, (slots, slots), 0)
+    coords = n_col * n_row
+    for copy in coords_copies:
+        copy.wait()
+    key = coords_v[0:1, :] * n_row + coords_v[8:9, :]
+    key_lane = jnp.where(lane < count[0, 0], jnp.broadcast_to(key, (slots, slots)), coords)
+    key_sub = jnp.transpose(key_lane)
+    same_before = jnp.sum(
+        ((key_lane == key_sub) & (lane < sub)).astype(jnp.int32), axis=1, keepdims=True
+    )
+    less = jnp.sum((key_lane < key_sub).astype(jnp.int32), axis=1, keepdims=True)
+    placed = (less + same_before) == lane
+    order = jnp.sum(jnp.where(placed, sub, 0), axis=0, keepdims=True)
+    keep = jnp.sum(
+        jnp.where(placed & (same_before > 0), 1, 0), axis=0, keepdims=True
+    )
+    upto = jnp.sum((key_sub <= lane).astype(jnp.int32), axis=0, keepdims=True)
+    here = jnp.sum((key_sub == lane).astype(jnp.int32), axis=0, keepdims=True)
+    last = jnp.where(here > 0, upto - 1, slots)
+    meta_v[0:1, :] = order
+    meta_v[1:2, :] = keep
+    meta_v[2:3, :] = last
+    meta_v[3:8, :] = jnp.zeros((5, slots), jnp.int32)
+    meta_copy = pltpu.make_async_copy(meta_v, meta_s, local_sem.at[2])
+    meta_copy.start()
+
     prefix[slots] = jnp.zeros((side, side), prefix.dtype)
     meta_copy.wait()
     adj_copy.wait()
@@ -168,12 +168,17 @@
     def send_parts(ch):
         @pl.when(at_end)
         def _():
-            sum_copy(ch, part.at[ch, along(3)], 3, 1, 0).start()
+            if ch == n_chunk - 1:
+                sum_copy(ch, part.at[ch, along(3)], 1, 3, 0).start()
+            else:
+                sum_copy(ch, part.at[ch, along(3)], 3, 1, 0).start()
             sum_copy(ch, part.at[ch, along(2)], 2, 2, 1).start()
             sum_copy(ch, part.at[ch, along(1)], 0, 1, 2).start()
 
         @pl.when(jnp.logical_not(at_end))
         def _():
+            if ch == n_chunk - 1:
+                sum_copy(ch, part.at[ch, along(3)], 3, 3, 0).start()
             sum_copy(ch, part.at[ch, along(2)], 1, 2, 1).start()
             sum_copy(ch, part.at[ch, along(0)], 0, 0, 2).start()
 
@@ -194,7 +199,11 @@
 
         @pl.when(at_end)
         def _():
-            agg[:, lanes] = total.astype(agg.dtype)
+            if ch == n_chunk - 1:
+                arrived(ch, 3)
+                agg[:, lanes] = (total + got[ch, 3].astype(jnp.float32)).astype(agg.dtype)
+            else:
+                agg[:, lanes] = total.astype(agg.dtype)
 
         @pl.when(jnp.logical_not(at_end))
         def _():
@@ -219,11 +228,10 @@
             product = piece if product is None else product + piece
         part[ch] = product.reshape(n_col, side, width).astype(part.dtype)
         send_parts(ch)
+        if ch >= 1:
+            pass_on(ch - 1)
         if ch + 1 < n_chunk:
             relay(ch + 1)
-        if ch >= 1:
-            pass_on(ch - 1)
-    pass_on(n_chunk - 1)
 
     for ch in range(n_chunk):
         finish(ch)

time: 28.6 us -> 28.5 us (level)
  no operation moved by 1% of the time
where the time goes in v4:
time: 28.5 us; the launch traced here: 28.3 us
  Pallas kernels  27 us (95%)
  between operations  1.29 us (5%)
    pallas_call x1, Pallas kernels, fused_body(): pl.pallas_call(functools.partial(fused_kernel, n_col), out_shape=jax.Shap...  24.5 us
    pallas_call x1, Pallas kernels, fused_body(): pl.pallas_call(project_kernel, out_shape=(jax.ShapeDtypeStruct((cells, fe...  2.55 us

profile of v4, /device:TPU:0, one launch (start us, length us, event | category | flops | bytes accessed | tf_op | source)
XLA Modules:
  0.0 28.3 jit_solution(8885668055347104729)
XLA Ops:
  1.3 24.5 %shard_map.77.agg = bf16[128,512]{1,0:T(8,128)(2,1)} custom-call(bf16[128,512]{1,0:T(8,128)(2,1)} %bitcast.5, bf16[128,128,128]{2,1,0:T(8,128)(2,1)} %bitcast.4, s32[1,128]{1,0:T(1,128)} %bitcast.6, s32[1,128]{1,0:T(1,128)} %bitcast.7, s32[1,1]{1,0:T(1,128)S(6)} %copy.8.count), custom_call_target="tpu_custom_call" | custom-call | tf_op jit(solution)/shard_map/pallas_call | solution.py:284
  25.8 2.5 %shard_map.78 = (bf16[128,512]{1,0:T(8,128)(2,1)}, bf16[128,1536]{1,0:T(8,128)(2,1)}) custom-call(bf16[128,512]{1,0:T(8,128)(2,1)} %shard_map.77.agg, bf16[512,1536]{1,0:T(8,128)(2,1)} %w.1), custom_call_target="tpu_custom_call" | custom-call | tf_op jit(solution)/shard_map/pallas_call | solution.py:311
